TPU v7x, 256 devices: a whole 4x4x8 slice. The times are simulated.
256 devices in a mesh: table: 16 (over y, x), blk: 16 (over z, core).
Axes of the slice: x: 4, y: 4, z: 8, core: 2. Of those that a mesh axis runs over, the one named last changes fastest.
Arguments:
- cold_table: bfloat16 [524288, 128], P('table'), may hold values from -6 to 6
- slot_row: int32 [4096, 2048], P(('table', 'blk')), may hold values from 0 to 32767
- slot_sample: int32 [4096, 2048], P(('table', 'blk')), may hold values from 0 to 511
- slot_count: int32 [4096, 2048], P(('table', 'blk')), may hold values from 0 to 15, as said below
- hot_table: bfloat16 [4096, 128], replicated, may hold values from -6 to 6
- hot_index: int32 [131072, 8], P(('table', 'blk')), may hold values from 0 to 4095
- hot_count: int32 [131072, 8], P(('table', 'blk')), may hold values from 1 to 15
- hot_cotangent: bfloat16 [131072, 128], P(('table', 'blk')), may hold values from -0.59765625 to 0.59765625
Outputs:
- features: bfloat16 [131072, 256], P(('table', 'blk'))
- hot_grad: float32 [4096, 128], P('blk')
Inputs may be any that keep to these rules, and one draw needn't show every extreme that they name: `slot_count`: slots of a bucket that carry no request have count 0 and follow its used slots; in every draw, for every index of blk, one cold shard receives 2048 used slots from every device with that index.
All inputs are finite; a program needn't handle non-finite values.
Results may differ from a plain program's by a relative error of at most 0.001.
Values may be sent and summed in bfloat16 or wider, within the bound.
No kernel may reach another device: no remote copies, remote signals or barrier semaphores. Data moves between devices by JAX's collectives and lax.ppermute only.
A program may use at most 128 MiB of HBM per device.

v0:
```python
import jax
import jax.numpy as jnp
from jax import lax
from jax.sharding import PartitionSpec as P

cold_scale = 0.03125
hot_scale = 0.0625


def incidence_pool(sample_idx, counts, picked, samples):
    matches = jnp.arange(samples, dtype=jnp.int32)[:, None] == sample_idx[None, :]
    weights = jnp.where(matches, counts[None, :].astype(jnp.float32) * cold_scale, 0.0).astype(
        jnp.bfloat16
    )
    return jnp.dot(weights, picked, preferred_element_type=jnp.float32)


def hot_incidence(hot_index, hot_count, hot_rows):
    row_ids = jnp.arange(hot_rows, dtype=jnp.int32)[None, :]
    hot_weights = hot_count.astype(jnp.float32) * hot_scale
    lookups = hot_index.shape[1]

    def add_lookup(step, total):
        index_col = lax.dynamic_slice_in_dim(hot_index, step, 1, 1)
        weight_col = lax.dynamic_slice_in_dim(hot_weights, step, 1, 1)
        return total + jnp.where(index_col == row_ids, weight_col, 0.0)

    empty = jnp.zeros((hot_index.shape[0], hot_rows), jnp.float32)
    return lax.fori_loop(0, lookups, add_lookup, empty).astype(jnp.bfloat16)


def shards(
    cold_table, slot_row, slot_sample, slot_count, hot_table, hot_index, hot_count, hot_cotangent
):
    samples = hot_index.shape[0]
    width = cold_table.shape[1]
    got_row = lax.all_to_all(slot_row, "table", split_axis=0, concat_axis=0, tiled=True)
    picked = jnp.take(cold_table, got_row, axis=0)
    returned = lax.all_to_all(picked, "table", split_axis=0, concat_axis=0, tiled=True)

    def add_owner(total, packed):
        return (total + incidence_pool(packed[0], packed[1], packed[2], samples), None)

    cold_pooled, _ = lax.scan(
        add_owner, jnp.zeros((samples, width), jnp.float32), (slot_sample, slot_count, returned)
    )
    hot_rows = hot_table.shape[0]
    incidence = hot_incidence(hot_index, hot_count, hot_rows)
    hot_pooled = jnp.dot(incidence, hot_table, preferred_element_type=jnp.float32)
    features = jnp.concatenate(
        [cold_pooled.astype(jnp.bfloat16), hot_pooled.astype(jnp.bfloat16)], axis=1
    )
    local_sums = lax.dot_general(
        incidence, hot_cotangent, (((0,), (0,)), ((), ())), preferred_element_type=jnp.float32
    )
    share_rows = lax.psum_scatter(local_sums, "blk", scatter_dimension=0, tiled=True)
    hot_grad = lax.psum(share_rows, "table")
    return (features, hot_grad)


def solution(mesh):
    return jax.shard_map(
        shards,
        mesh=mesh,
        in_specs=(
            P("table", None),
            P(("table", "blk"), None),
            P(("table", "blk"), None),
            P(("table", "blk"), None),
            P(),
            P(("table", "blk"), None),
            P(("table", "blk"), None),
            P(("table", "blk"), None),
        ),
        out_specs=(P(("table", "blk"), None), P("blk", None)),
        check_vma=False,
    )
```

profile of v0, /device:TPU:2, one launch (start us, length us, event | category | flops | bytes accessed | tf_op | source)
XLA Modules:
  0.0 381.2 jit_solution(16679746886880917182)
XLA Ops:
  8.9 7.5 %all-to-all-start = ((s32[16,1,2048]{2,1,0:T(1,128)}), s32[16,1,2048]{2,1,0:T(1,128)S(1)}, u32[]{:S(2)}, u32[]{:S(2)}) async-start(s32[16,1,2048]{2,1,0:T(1,128)} %all_to_all.13), calls=%async_computation | async-start | bytes 262144 | tf_op jit(solution)/shard_map/all_to_all | solution.py:37
  17.1 5.9 %all-to-all-done = s32[16,1,2048]{2,1,0:T(1,128)S(1)} async-done(((s32[16,1,2048]{2,1,0:T(1,128)}), s32[16,1,2048]{2,1,0:T(1,128)S(1)}, u32[]{:S(2)}, u32[]{:S(2)}) %all-to-all-start) | async-done | bytes 131104 | tf_op jit(solution)/shard_map/all_to_all | solution.py:37
  23.2 114.6 %gather_fusion = bf16[32768,128]{1,0:T(8,128)(2,1)} fusion(bf16[32768,128]{1,0:T(8,128)(2,1)} %param.12, s32[32768]{0:T(1024)S(1)} %broadcast_clamp_fusion), kind=kCustom, calls=%fused_computation | custom fusion | bytes 16908288 | tf_op jit(solution)/shard_map/jit(_take)/gather | solution.py:38
  137.9 7.9 %broadcast_select_fusion = bf16[16,2048,128]{2,1,0:T(8,128)(2,1)} fusion(bf16[16,2048,128]{2,1,0:T(8,128)(2,1)} %bitcast.27, pred[16,2048]{1,0:T(8,128)(4,1)S(1)} %compare_and_fusion), kind=kLoop, calls=%fused_computation.19 | loop fusion | flops 4194304 | bytes 16809984 | tf_op jit(solution)/shard_map/jit(_take)/select_n | solution.py:38
  145.8 6.0 %all-to-all-start.1 = ((bf16[16,2048,128]{2,1,0:T(8,128)(2,1)}), bf16[16,2048,128]{2,1,0:T(8,128)(2,1)}, u32[]{:S(2)}, u32[]{:S(2)}) async-start(bf16[16,2048,128]{2,1,0:T(8,128)(2,1)} %broadcast_select_fusion), calls=%async_computation.1 | async-start | bytes 16777216 | tf_op jit(solution)/shard_map/all_to_all | solution.py:39
  151.8 56.0 %while.26 = (s32[]{:T(128)}, f32[512,4096]{1,0:T(8,128)}, s32[512,8]{0,1:T(8,128)}, f32[512,8]{0,1:T(8,128)S(1)}, s32[]{:T(128)}, /*index=5*/s32[]{:T(128)}) while((s32[]{:T(128)}, f32[512,4096]{1,0:T(8,128)}, s32[512,8]{0,1:T(8,128)}, f32[512,8]{0,1:T(8,128)S(1)}, s32[]{:T(128)}, /*index=5*/s32[]{:T(128)}) %tuple.55), condition=%wide.region_3.4_spmd.clone, body=%wide.region_2.3_spmd.clone.sunk | while | flops 8388611 | bytes 16789588 | solution.py:29
  152.6 4.4 %select_add_fusion.2 = f32[512,4096]{1,0:T(8,128)} fusion(f32[512,4096]{1,0:T(8,128)} %get-tuple-element.245, f32[512]{0:T(512)S(1)} %bitcast.29, s32[512]{0:T(512)S(1)} %bitcast.30, pred[]{:T(512)S(6)} %compare.7), kind=kLoop, calls=%fused_computation.16.clone.1 | loop fusion | flops 8388608 | bytes 16781312 | tf_op jit(solution)/shard_map/while/body/eval_jaxpr/add | solution.py:26
  157.6 6.5 %select_add_fusion.2 = f32[512,4096]{1,0:T(8,128)} fusion(f32[512,4096]{1,0:T(8,128)} %get-tuple-element.245, f32[512]{0:T(512)S(1)} %bitcast.29, s32[512]{0:T(512)S(1)} %bitcast.30, pred[]{:T(512)S(6)} %compare.7), kind=kLoop, calls=%fused_computation.16.clone.1 | loop fusion | flops 8388608 | bytes 16781312 | tf_op jit(solution)/shard_map/while/body/eval_jaxpr/add | solution.py:26
  164.9 6.5 %select_add_fusion.2 = f32[512,4096]{1,0:T(8,128)} fusion(f32[512,4096]{1,0:T(8,128)} %get-tuple-element.245, f32[512]{0:T(512)S(1)} %bitcast.29, s32[512]{0:T(512)S(1)} %bitcast.30, pred[]{:T(512)S(6)} %compare.7), kind=kLoop, calls=%fused_computation.16.clone.1 | loop fusion | flops 8388608 | bytes 16781312 | tf_op jit(solution)/shard_map/while/body/eval_jaxpr/add | solution.py:26
  172.2 6.5 %select_add_fusion.2 = f32[512,4096]{1,0:T(8,128)} fusion(f32[512,4096]{1,0:T(8,128)} %get-tuple-element.245, f32[512]{0:T(512)S(1)} %bitcast.29, s32[512]{0:T(512)S(1)} %bitcast.30, pred[]{:T(512)S(6)} %compare.7), kind=kLoop, calls=%fused_computation.16.clone.1 | loop fusion | flops 8388608 | bytes 16781312 | tf_op jit(solution)/shard_map/while/body/eval_jaxpr/add | solution.py:26
  179.4 6.5 %select_add_fusion.2 = f32[512,4096]{1,0:T(8,128)} fusion(f32[512,4096]{1,0:T(8,128)} %get-tuple-element.245, f32[512]{0:T(512)S(1)} %bitcast.29, s32[512]{0:T(512)S(1)} %bitcast.30, pred[]{:T(512)S(6)} %compare.7), kind=kLoop, calls=%fused_computation.16.clone.1 | loop fusion | flops 8388608 | bytes 16781312 | tf_op jit(solution)/shard_map/while/body/eval_jaxpr/add | solution.py:26
  186.7 6.5 %select_add_fusion.2 = f32[512,4096]{1,0:T(8,128)} fusion(f32[512,4096]{1,0:T(8,128)} %get-tuple-element.245, f32[512]{0:T(512)S(1)} %bitcast.29, s32[512]{0:T(512)S(1)} %bitcast.30, pred[]{:T(512)S(6)} %compare.7), kind=kLoop, calls=%fused_computation.16.clone.1 | loop fusion | flops 8388608 | bytes 16781312 | tf_op jit(solution)/shard_map/while/body/eval_jaxpr/add | solution.py:26
  194.0 6.5 %select_add_fusion.2 = f32[512,4096]{1,0:T(8,128)} fusion(f32[512,4096]{1,0:T(8,128)} %get-tuple-element.245, f32[512]{0:T(512)S(1)} %bitcast.29, s32[512]{0:T(512)S(1)} %bitcast.30, pred[]{:T(512)S(6)} %compare.7), kind=kLoop, calls=%fused_computation.16.clone.1 | loop fusion | flops 8388608 | bytes 16781312 | tf_op jit(solution)/shard_map/while/body/eval_jaxpr/add | solution.py:26
  201.2 6.5 %select_add_fusion.2 = f32[512,4096]{1,0:T(8,128)} fusion(f32[512,4096]{1,0:T(8,128)} %get-tuple-element.245, f32[512]{0:T(512)S(1)} %bitcast.29, s32[512]{0:T(512)S(1)} %bitcast.30, pred[]{:T(512)S(6)} %compare.7), kind=kLoop, calls=%fused_computation.16.clone.1 | loop fusion | flops 8388608 | bytes 16781312 | tf_op jit(solution)/shard_map/while/body/eval_jaxpr/add | solution.py:26
  207.7 6.0 %fusion.11 = f32[4096,128]{1,0:T(8,128)} fusion(bf16[512,128]{1,0:T(8,128)(2,1)S(1)} %copy-done.1, f32[512,4096]{1,0:T(8,128)} %get-tuple-element.124), kind=kOutput, calls=%fused_computation.20 | convolution fusion | flops 538968064 | bytes 10616832 | tf_op jit(solution)/shard_map/dot_general | solution.py:53
  213.9 4.9 %fusion.15 = bf16[512,128]{0,1:T(8,128)(2,1)S(1)} fusion(bf16[4096,128]{1,0:T(8,128)(2,1)S(1)} %copy-done, f32[512,4096]{1,0:T(8,128)} %get-tuple-element.124), kind=kOutput, calls=%fused_computation.24 | convolution fusion | flops 539033600 | bytes 9568256 | tf_op jit(solution)/shard_map/dot_general | solution.py:49
  218.8 58.8 %reduce-scatter.2.cloned.1.call-done = f32[256,128]{1,0:T(8,128)} async-done(((f32[4096,128]{1,0:T(8,128)}), f32[256,128]{1,0:T(8,128)}) %reduce-scatter.2.cloned.1.call-update) | async-done | bytes 131088 | tf_op jit(solution)/shard_map/reduce_scatter | solution.py:56
  277.6 56.7 %while.25 = (s32[]{:T(128)}, f32[512,128]{1,0:T(8,128)S(1)}, s32[16,2048]{1,0:T(8,128)}, s32[16,2048]{1,0:T(8,128)}, bf16[16,2048,128]{2,1,0:T(8,128)(2,1)}, /*index=5*/s32[]{:T(128)}, s32[]{:T(128)}) while((s32[]{:T(128)}, f32[512,128]{1,0:T(8,128)S(1)}, s32[16,2048]{1,0:T(8,128)}, s32[16,2048]{1,0:T(8,128)}, ...), condition=%wide.region_1.2_spmd.clone, body=%wide.region_0.1_spmd.clone.sunk | while | flops 270667776 | bytes 1098335 | solution.py:44
  279.4 1.8 fusion.23
  282.9 1.8 fusion.23
  286.4 1.8 fusion.23
  290.0 1.8 fusion.23
  293.5 1.8 fusion.23
  297.1 1.8 fusion.23
  304.2 1.8 fusion.23
  311.3 1.8 fusion.23
  314.8 1.8 fusion.23
  321.9 1.8 fusion.23
  325.4 1.8 fusion.23
  329.0 1.8 fusion.23
  332.5 1.8 fusion.23
  335.3 37.5 %all-reduce.2.cloned.1.call-done = f32[256,128]{1,0:T(8,128)} async-done(((f32[256,128]{1,0:T(8,128)}), f32[256,128]{1,0:T(8,128)}) %all-reduce.2.cloned.1.call-update) | async-done | bytes 131088 | tf_op jit(solution)/shard_map/psum | solution.py:57
  (71 shorter events, 44.0 us)
Async XLA Ops:
  7.2 206.7 %copy-start = (bf16[4096,128]{1,0:T(8,128)(2,1)S(1)}, bf16[4096,128]{1,0:T(8,128)(2,1)}, u32[]{:S(2)}) copy-start(bf16[4096,128]{1,0:T(8,128)(2,1)} %param.16) | copy-start | bytes 3145732
  8.9 14.1 %all-to-all-start = ((s32[16,1,2048]{2,1,0:T(1,128)}), s32[16,1,2048]{2,1,0:T(1,128)S(1)}, u32[]{:S(2)}, u32[]{:S(2)}) async-start(s32[16,1,2048]{2,1,0:T(1,128)} %all_to_all.13), calls=%async_computation | async-start | bytes 262144 | tf_op jit(solution)/shard_map/all_to_all | solution.py:37
  145.8 131.9 %all-to-all-start.1 = ((bf16[16,2048,128]{2,1,0:T(8,128)(2,1)}), bf16[16,2048,128]{2,1,0:T(8,128)(2,1)}, u32[]{:S(2)}, u32[]{:S(2)}) async-start(bf16[16,2048,128]{2,1,0:T(8,128)(2,1)} %broadcast_select_fusion), calls=%async_computation.1 | async-start | bytes 16777216 | tf_op jit(solution)/shard_map/all_to_all | solution.py:39
  151.7 125.9 %reduce-scatter.2.cloned.1.call-start = ((), (), s32[]{:S(2)}) async-start(), calls=%async_computation.3 | async-start | bytes 2228224 | tf_op jit(solution)/shard_map/reduce_scatter | solution.py:56
  151.8 56.0 %copy-start.1 = (bf16[512,128]{1,0:T(8,128)(2,1)S(1)}, bf16[512,128]{1,0:T(8,128)(2,1)}, u32[]{:S(2)}) copy-start(bf16[512,128]{1,0:T(8,128)(2,1)} %param.19) | copy-start | bytes 393220
  213.8 159.0 %all-reduce.2.cloned.1.call-start = ((), (), s32[]{:S(2)}) async-start(), calls=%async_computation.4 | async-start | bytes 262144 | tf_op jit(solution)/shard_map/psum | solution.py:57
Sparse Core Ops, SparseCore 0:
  213.9 63.6 reduce-scatter.1
  280.8 92.0 all-reduce.1
where the time goes:
time: 384 us; the launch traced here: 381 us
  local copies, waits for them, and re-layouts  138 us (36%)
  waiting for transfers between devices  102 us (27%)
  other arithmetic  72.6 us (19%)
  matrix products  39.8 us (10%)
  between operations  14.1 us (4%)
  starting transfers between devices  13.5 us (4%)
    gather x1, local copies, waits for them, and re-layouts, shards(): picked = jnp.take(cold_table, got_row, axis=0)  115 us
    reduce_scatter x1, waiting for transfers between devices, shards(): lax.psum_scatter(local_sums, 'blk', scatter_dimension=0, tiled=True)  58.8 us
    add x8, other arithmetic, add_lookup(): return total + jnp.where(index_col == row_ids, weight_col, 0.0)  50.1 us
    psum x1, waiting for transfers between devices, shards(): hot_grad = lax.psum(share_rows, 'table')  37.5 us
    dot_general x16, matrix products, incidence_pool(): return jnp.dot(weights, picked, preferred_element_type=jnp.float32)  28.9 us
    mul x16, other arithmetic, incidence_pool(): counts[None, :].astype(jnp.float32) * cold_scale  13.7 us
    dynamic_slice x16, local copies, waits for them, and re-layouts, shards(): lax.scan(add_owner, jnp.zeros((samples, width), jnp.float32), (slot_sampl...  13.7 us
    select_n x2, other arithmetic, shards(): picked = jnp.take(cold_table, got_row, axis=0)  8.02 us
  transfers between devices with their start and end apart: 4, of which 3 were waited for; matrix products, arithmetic and copies ran while one was open for 33% of the time, Pallas kernels for 0%

commit v1 on v0

--- a/solution.py
+++ b/solution.py
@@ -5,6 +5,12 @@
 
 cold_scale = 0.03125
 hot_scale = 0.0625
+
+
+def add_all(x, mesh_axis):
+    pieces = lax.all_gather(x, mesh_axis, axis=0, tiled=False)
+    total = pieces.sum(axis=0)
+    return total
 
 
 def incidence_pool(sample_idx, counts, picked, samples):
@@ -54,7 +60,7 @@
         incidence, hot_cotangent, (((0,), (0,)), ((), ())), preferred_element_type=jnp.float32
     )
     share_rows = lax.psum_scatter(local_sums, "blk", scatter_dimension=0, tiled=True)
-    hot_grad = lax.psum(share_rows, "table")
+    hot_grad = add_all(share_rows, "table")
     return (features, hot_grad)
 
 

time: 384 us -> 349 us (0.909)
  waiting for transfers between devices: 102 us -> 64.8 us
    psum x1 -> x0, waiting for transfers between devices: 37.5 us -> none  [shards(): hot_grad = lax.psum(share_rows, 'table')]
  transfers between devices with their start and end apart: 4 -> 4, of which waited for: 3 -> 2; matrix products, arithmetic and copies ran while one was open for 33% -> 36% of each run, Pallas kernels for 0% -> 0%
where the time goes in v1:
time: 349 us; the launch traced here: 345 us
  local copies, waits for them, and re-layouts  137 us (39%)
  other arithmetic  75 us (21%)
  waiting for transfers between devices  64.8 us (19%)
  matrix products  39.8 us (11%)
  between operations  14.1 us (4%)
  starting transfers between devices  13.5 us (4%)
    gather x1, local copies, waits for them, and re-layouts, shards(): picked = jnp.take(cold_table, got_row, axis=0)  115 us
    reduce_scatter x1, waiting for transfers between devices, shards(): lax.psum_scatter(local_sums, 'blk', scatter_dimension=0, tiled=True)  58.8 us
    add x8, other arithmetic, add_lookup(): return total + jnp.where(index_col == row_ids, weight_col, 0.0)  50.1 us
    dot_general x16, matrix products, incidence_pool(): return jnp.dot(weights, picked, preferred_element_type=jnp.float32)  28.9 us
    mul x16, other arithmetic, incidence_pool(): counts[None, :].astype(jnp.float32) * cold_scale  13.7 us
    dynamic_slice x16, local copies, waits for them, and re-layouts, shards(): lax.scan(add_owner, jnp.zeros((samples, width), jnp.float32), (slot_sampl...  13.7 us
    select_n x2, other arithmetic, shards(): picked = jnp.take(cold_table, got_row, axis=0)  8.02 us
    all_to_all x1, starting transfers between devices, shards(): lax.all_to_all(slot_row, 'table', split_axis=0, concat_axis=0, tiled=True)  7.48 us
  transfers between devices with their start and end apart: 4, of which 2 were waited for; matrix products, arithmetic and copies ran while one was open for 36% of the time, Pallas kernels for 0%

profile of v1, /device:TPU:2, one launch (start us, length us, event | category | flops | bytes accessed | tf_op | source)
XLA Modules:
  0.0 344.5 jit_solution(14211295256408409577)
XLA Ops:
  8.9 7.5 %all-to-all-start = ((s32[16,1,2048]{2,1,0:T(1,128)}), s32[16,1,2048]{2,1,0:T(1,128)S(1)}, u32[]{:S(2)}, u32[]{:S(2)}) async-start(s32[16,1,2048]{2,1,0:T(1,128)} %all_to_all.13), calls=%async_computation | async-start | bytes 262144 | tf_op jit(solution)/shard_map/all_to_all | solution.py:43
  17.1 5.9 %all-to-all-done = s32[16,1,2048]{2,1,0:T(1,128)S(1)} async-done(((s32[16,1,2048]{2,1,0:T(1,128)}), s32[16,1,2048]{2,1,0:T(1,128)S(1)}, u32[]{:S(2)}, u32[]{:S(2)}) %all-to-all-start) | async-done | bytes 131104 | tf_op jit(solution)/shard_map/all_to_all | solution.py:43
  23.2 114.6 %gather_fusion = bf16[32768,128]{1,0:T(8,128)(2,1)} fusion(bf16[32768,128]{1,0:T(8,128)(2,1)} %param.12, s32[32768]{0:T(1024)S(1)} %broadcast_clamp_fusion), kind=kCustom, calls=%fused_computation | custom fusion | bytes 16908288 | tf_op jit(solution)/shard_map/jit(_take)/gather | solution.py:44
  137.9 7.9 %broadcast_select_fusion = bf16[16,2048,128]{2,1,0:T(8,128)(2,1)} fusion(bf16[16,2048,128]{2,1,0:T(8,128)(2,1)} %bitcast.28, pred[16,2048]{1,0:T(8,128)(4,1)S(1)} %compare_and_fusion), kind=kLoop, calls=%fused_computation.19 | loop fusion | flops 4194304 | bytes 16809984 | tf_op jit(solution)/shard_map/jit(_take)/select_n | solution.py:44
  145.8 6.0 %all-to-all-start.1 = ((bf16[16,2048,128]{2,1,0:T(8,128)(2,1)}), bf16[16,2048,128]{2,1,0:T(8,128)(2,1)}, u32[]{:S(2)}, u32[]{:S(2)}) async-start(bf16[16,2048,128]{2,1,0:T(8,128)(2,1)} %broadcast_select_fusion), calls=%async_computation.1 | async-start | bytes 16777216 | tf_op jit(solution)/shard_map/all_to_all | solution.py:45
  151.8 56.0 %while.26 = (s32[]{:T(128)}, f32[512,4096]{1,0:T(8,128)}, s32[512,8]{0,1:T(8,128)}, f32[512,8]{0,1:T(8,128)S(1)}, s32[]{:T(128)}, /*index=5*/s32[]{:T(128)}) while((s32[]{:T(128)}, f32[512,4096]{1,0:T(8,128)}, s32[512,8]{0,1:T(8,128)}, f32[512,8]{0,1:T(8,128)S(1)}, s32[]{:T(128)}, /*index=5*/s32[]{:T(128)}) %tuple.55), condition=%wide.region_3.4_spmd.clone, body=%wide.region_2.3_spmd.clone.sunk | while | flops 8388611 | bytes 16789588 | solution.py:35
  152.6 4.4 %select_add_fusion.2 = f32[512,4096]{1,0:T(8,128)} fusion(f32[512,4096]{1,0:T(8,128)} %get-tuple-element.245, f32[512]{0:T(512)S(1)} %bitcast.31, s32[512]{0:T(512)S(1)} %bitcast.32, pred[]{:T(512)S(6)} %compare.7), kind=kLoop, calls=%fused_computation.16.clone.1 | loop fusion | flops 8388608 | bytes 16781312 | tf_op jit(solution)/shard_map/while/body/eval_jaxpr/add | solution.py:32
  157.6 6.5 %select_add_fusion.2 = f32[512,4096]{1,0:T(8,128)} fusion(f32[512,4096]{1,0:T(8,128)} %get-tuple-element.245, f32[512]{0:T(512)S(1)} %bitcast.31, s32[512]{0:T(512)S(1)} %bitcast.32, pred[]{:T(512)S(6)} %compare.7), kind=kLoop, calls=%fused_computation.16.clone.1 | loop fusion | flops 8388608 | bytes 16781312 | tf_op jit(solution)/shard_map/while/body/eval_jaxpr/add | solution.py:32
  164.9 6.5 %select_add_fusion.2 = f32[512,4096]{1,0:T(8,128)} fusion(f32[512,4096]{1,0:T(8,128)} %get-tuple-element.245, f32[512]{0:T(512)S(1)} %bitcast.31, s32[512]{0:T(512)S(1)} %bitcast.32, pred[]{:T(512)S(6)} %compare.7), kind=kLoop, calls=%fused_computation.16.clone.1 | loop fusion | flops 8388608 | bytes 16781312 | tf_op jit(solution)/shard_map/while/body/eval_jaxpr/add | solution.py:32
  172.2 6.5 %select_add_fusion.2 = f32[512,4096]{1,0:T(8,128)} fusion(f32[512,4096]{1,0:T(8,128)} %get-tuple-element.245, f32[512]{0:T(512)S(1)} %bitcast.31, s32[512]{0:T(512)S(1)} %bitcast.32, pred[]{:T(512)S(6)} %compare.7), kind=kLoop, calls=%fused_computation.16.clone.1 | loop fusion | flops 8388608 | bytes 16781312 | tf_op jit(solution)/shard_map/while/body/eval_jaxpr/add | solution.py:32
  179.4 6.5 %select_add_fusion.2 = f32[512,4096]{1,0:T(8,128)} fusion(f32[512,4096]{1,0:T(8,128)} %get-tuple-element.245, f32[512]{0:T(512)S(1)} %bitcast.31, s32[512]{0:T(512)S(1)} %bitcast.32, pred[]{:T(512)S(6)} %compare.7), kind=kLoop, calls=%fused_computation.16.clone.1 | loop fusion | flops 8388608 | bytes 16781312 | tf_op jit(solution)/shard_map/while/body/eval_jaxpr/add | solution.py:32
  186.7 6.5 %select_add_fusion.2 = f32[512,4096]{1,0:T(8,128)} fusion(f32[512,4096]{1,0:T(8,128)} %get-tuple-element.245, f32[512]{0:T(512)S(1)} %bitcast.31, s32[512]{0:T(512)S(1)} %bitcast.32, pred[]{:T(512)S(6)} %compare.7), kind=kLoop, calls=%fused_computation.16.clone.1 | loop fusion | flops 8388608 | bytes 16781312 | tf_op jit(solution)/shard_map/while/body/eval_jaxpr/add | solution.py:32
  194.0 6.5 %select_add_fusion.2 = f32[512,4096]{1,0:T(8,128)} fusion(f32[512,4096]{1,0:T(8,128)} %get-tuple-element.245, f32[512]{0:T(512)S(1)} %bitcast.31, s32[512]{0:T(512)S(1)} %bitcast.32, pred[]{:T(512)S(6)} %compare.7), kind=kLoop, calls=%fused_computation.16.clone.1 | loop fusion | flops 8388608 | bytes 16781312 | tf_op jit(solution)/shard_map/while/body/eval_jaxpr/add | solution.py:32
  201.2 6.5 %select_add_fusion.2 = f32[512,4096]{1,0:T(8,128)} fusion(f32[512,4096]{1,0:T(8,128)} %get-tuple-element.245, f32[512]{0:T(512)S(1)} %bitcast.31, s32[512]{0:T(512)S(1)} %bitcast.32, pred[]{:T(512)S(6)} %compare.7), kind=kLoop, calls=%fused_computation.16.clone.1 | loop fusion | flops 8388608 | bytes 16781312 | tf_op jit(solution)/shard_map/while/body/eval_jaxpr/add | solution.py:32
  207.7 6.0 %fusion.11 = f32[4096,128]{1,0:T(8,128)} fusion(bf16[512,128]{1,0:T(8,128)(2,1)S(1)} %copy-done.1, f32[512,4096]{1,0:T(8,128)} %get-tuple-element.124), kind=kOutput, calls=%fused_computation.20 | convolution fusion | flops 538968064 | bytes 10616832 | tf_op jit(solution)/shard_map/dot_general | solution.py:59
  213.9 4.9 %fusion.15 = bf16[512,128]{0,1:T(8,128)(2,1)S(1)} fusion(bf16[4096,128]{1,0:T(8,128)(2,1)S(1)} %copy-done, f32[512,4096]{1,0:T(8,128)} %get-tuple-element.124), kind=kOutput, calls=%fused_computation.24 | convolution fusion | flops 539033600 | bytes 9568256 | tf_op jit(solution)/shard_map/dot_general | solution.py:55
  218.8 58.8 %reduce-scatter.2.cloned.1.call-done = f32[256,128]{1,0:T(8,128)} async-done(((f32[4096,128]{1,0:T(8,128)}), f32[256,128]{1,0:T(8,128)}) %reduce-scatter.2.cloned.1.call-update) | async-done | bytes 131088 | tf_op jit(solution)/shard_map/reduce_scatter | solution.py:62
  277.6 56.7 %while.25 = (s32[]{:T(128)}, f32[512,128]{1,0:T(8,128)S(1)}, s32[16,2048]{1,0:T(8,128)}, s32[16,2048]{1,0:T(8,128)}, bf16[16,2048,128]{2,1,0:T(8,128)(2,1)}, /*index=5*/s32[]{:T(128)}, s32[]{:T(128)}) while((s32[]{:T(128)}, f32[512,128]{1,0:T(8,128)S(1)}, s32[16,2048]{1,0:T(8,128)}, s32[16,2048]{1,0:T(8,128)}, ...), condition=%wide.region_1.2_spmd.clone, body=%wide.region_0.1_spmd.clone.sunk | while | flops 270667776 | bytes 1098335 | solution.py:50
  279.4 1.8 fusion.23
  286.4 1.8 fusion.23
  290.0 1.8 fusion.23
  293.5 1.8 fusion.23
  297.1 1.8 fusion.23
  300.6 1.8 fusion.23
  304.2 1.8 fusion.23
  307.7 1.8 fusion.23
  311.2 1.8 fusion.23
  314.8 1.8 fusion.23
  321.9 1.8 fusion.23
  325.4 1.8 fusion.23
  329.0 1.8 fusion.23
  335.3 2.4 reduce_sum.9
  (71 shorter events, 42.5 us)
Async XLA Ops:
  7.2 206.7 %copy-start = (bf16[4096,128]{1,0:T(8,128)(2,1)S(1)}, bf16[4096,128]{1,0:T(8,128)(2,1)}, u32[]{:S(2)}) copy-start(bf16[4096,128]{1,0:T(8,128)(2,1)} %param.16) | copy-start | bytes 3145732
  8.9 14.1 %all-to-all-start = ((s32[16,1,2048]{2,1,0:T(1,128)}), s32[16,1,2048]{2,1,0:T(1,128)S(1)}, u32[]{:S(2)}, u32[]{:S(2)}) async-start(s32[16,1,2048]{2,1,0:T(1,128)} %all_to_all.13), calls=%async_computation | async-start | bytes 262144 | tf_op jit(solution)/shard_map/all_to_all | solution.py:43
  145.8 131.9 %all-to-all-start.1 = ((bf16[16,2048,128]{2,1,0:T(8,128)(2,1)}), bf16[16,2048,128]{2,1,0:T(8,128)(2,1)}, u32[]{:S(2)}, u32[]{:S(2)}) async-start(bf16[16,2048,128]{2,1,0:T(8,128)(2,1)} %broadcast_select_fusion), calls=%async_computation.1 | async-start | bytes 16777216 | tf_op jit(solution)/shard_map/all_to_all | solution.py:45
  151.7 125.9 %reduce-scatter.2.cloned.1.call-start = ((), (), s32[]{:S(2)}) async-start(), calls=%async_computation.3 | async-start | bytes 2228224 | tf_op jit(solution)/shard_map/reduce_scatter | solution.py:62
  151.8 56.0 %copy-start.1 = (bf16[512,128]{1,0:T(8,128)(2,1)S(1)}, bf16[512,128]{1,0:T(8,128)(2,1)}, u32[]{:S(2)}) copy-start(bf16[512,128]{1,0:T(8,128)(2,1)} %param.19) | copy-start | bytes 393220
  213.8 121.5 %all-gather.3.cloned.1.call-start = ((), (), s32[]{:S(2)}) async-start(), calls=%async_computation.4 | async-start | bytes 2228224 | tf_op jit(solution)/shard_map/all_gather | solution.py:11
Sparse Core Ops, SparseCore 0:
  213.9 63.6 reduce-scatter.1
  280.0 48.7 all-gather.2
